TPU v7x, 32 devices: a whole 2x2x4 slice. The times are simulated.
32 devices in a mesh: row: 8 (over z, y), col: 4 (over x, core).
Axes of the slice: x: 2, y: 2, z: 4, core: 2. Of those that a mesh axis runs over, the one named last changes fastest.
Arguments:
- image_states: bfloat16 [64, 3072], P(('row', 'col')), may hold values from -6 to 6
- latent: float32 [64, 64], P(('row', 'col')), may hold values from -6 to 6
- text_keys: bfloat16 [1024, 3072], P('row', 'col')
- text_values: bfloat16 [1024, 3072], P('row', 'col'), may hold values from -6 to 6
- mod_table: float32 [4, 8, 3072], replicated, may hold values from -3 to 3
- timestep: int32 [4], replicated, may hold values from 0 to 3
- grid_size: int32 [4, 2], replicated, may hold values from 1 to 8, as said below
- rope_offset: int32 [4, 2], replicated, may hold values from 0 to 63
- w_qkv: bfloat16 [3072, 9216], P(None, 'row'), may hold values from -0.109375 to 0.109375
- q_gain: float32 [128], replicated, may hold values from 0.1 to 1.9
- k_gain: float32 [128], replicated, may hold values from 0.5 to 4
- w_out: bfloat16 [3072, 3072], P('col', 'row'), may hold values from -0.109375 to 0.109375
- w_fc1: bfloat16 [3072, 12288], P(None, 'row'), may hold values from -0.109375 to 0.109375
- w_fc2: bfloat16 [12288, 3072], P('row'), may hold values from -0.0546875 to 0.0546875
- w_final: bfloat16 [3072, 64], replicated, may hold values from -0.109375 to 0.109375
Outputs:
- velocity: float32 [64, 64], P(('row', 'col'))
- next_latent: float32 [64, 64], P(('row', 'col'))
Inputs may be any that keep to these rules, and one draw needn't show every extreme that they name: `grid_size`: column 0 is a request's grid height, at most 2; column 1 its grid width, at most 8; in every draw some request has height 2 and some request width 8.
All inputs are finite; a program needn't handle non-finite values.
Results may differ from a plain program's by a relative error of at most 0.008.
Values may be sent and summed in bfloat16 or wider, within the bound.
No kernel may reach another device: no remote copies, remote signals or barrier semaphores. Data moves between devices by JAX's collectives and lax.ppermute only.
A program may use at most 128 MiB of HBM per device.

v0:
```python
import jax
import jax.numpy as jnp
from jax import lax
from jax.sharding import PartitionSpec as P

REQ = 4
TXT = 256
STEPS = 4
eps_norm = 1e-06
blend = 0.25
mask_floor = -1e30


def with_halo(cells, sides, width):
    for axis, dim in sides:
        count = lax.axis_size(axis)
        ends = count - 1
        head = lax.slice_in_dim(cells, 0, width, axis=dim)
        tail = lax.slice_in_dim(cells, cells.shape[dim] - width, cells.shape[dim], axis=dim)
        cells = jnp.concatenate(
            [
                lax.ppermute(tail, axis, [(i, (i + 1) % count) for i in range(ends)]),
                cells,
                lax.ppermute(head, axis, [((i + 1) % count, i) for i in range(ends)]),
            ],
            axis=dim,
        )
    return cells


def layer_norm(values):
    mean_value = jnp.mean(values, -1, keepdims=True)
    centred = values - mean_value
    return centred * lax.rsqrt(jnp.mean(centred * centred, -1, keepdims=True) + eps_norm)


def modulate(values, shift_vec, scale_vec):
    return (layer_norm(values) * (1.0 + scale_vec) + shift_vec).astype(jnp.bfloat16)


def rope_tables(pos_h, pos_w, head_size):
    time_half = head_size // 16
    axis_dim = (head_size - head_size // 8) // 2
    freq_index = jnp.arange(axis_dim // 2, dtype=jnp.float32)
    frequency = 10000.0 ** (-2.0 * freq_index / axis_dim)
    angles = jnp.concatenate(
        [
            jnp.zeros((pos_h.shape[0], time_half), jnp.float32),
            pos_h[:, None] * frequency[None, :],
            pos_w[:, None] * frequency[None, :],
        ],
        1,
    )
    return (jnp.cos(angles), jnp.sin(angles))


def norm_rope(values, gain_vec, cosine_table, sine_table, head_count, head_size):
    row_total = values.shape[0]
    per_head = values.astype(jnp.float32).reshape(row_total, head_count, head_size)
    per_head = (
        per_head * lax.rsqrt(jnp.mean(per_head * per_head, -1, keepdims=True) + eps_norm) * gain_vec
    )
    paired = per_head.reshape(row_total, head_count, head_size // 2, 2)
    even_part = paired[..., 0]
    odd_part = paired[..., 1]
    cos_wide = cosine_table[:, None, :]
    sin_wide = sine_table[:, None, :]
    turned = jnp.stack(
        [even_part * cos_wide - odd_part * sin_wide, even_part * sin_wide + odd_part * cos_wide], -1
    )
    return turned.reshape(row_total, head_count * head_size).astype(jnp.bfloat16)


def on_device(
    image_states,
    latent,
    text_keys,
    text_values,
    mod_table,
    timestep,
    grid_size,
    rope_offset,
    w_qkv,
    q_gain,
    k_gain,
    w_out,
    w_fc1,
    w_fc2,
    w_final,
):
    col_total = lax.axis_size("col")
    row_pos = lax.axis_index("row")
    col_pos = lax.axis_index("col")
    tile_w = image_states.shape[0]
    width = image_states.shape[1]
    head_size = q_gain.shape[0]
    head_count = width // head_size
    local_heads = head_count // col_total
    request = row_pos % REQ
    grid_row = row_pos // REQ
    grid_col = col_pos * tile_w + jnp.arange(tile_w, dtype=jnp.int32)
    req_slots = jnp.arange(REQ, dtype=jnp.int32)
    req_onehot = req_slots == request
    limits = jnp.sum(jnp.where(req_onehot[:, None], grid_size, 0), 0)
    offsets = jnp.sum(jnp.where(req_onehot[:, None], rope_offset, 0), 0)
    step_now = jnp.sum(jnp.where(req_onehot, timestep, 0))
    token_ok = (grid_row < limits[0]) & (grid_col < limits[1])
    modulation = lax.dynamic_index_in_dim(mod_table, step_now, 0, keepdims=False)
    states = image_states.astype(jnp.float32)
    normed = modulate(states, modulation[0], modulation[1])
    joined_cols = jnp.dot(
        lax.all_gather(normed, "row", axis=0, tiled=True), w_qkv, preferred_element_type=jnp.float32
    ).astype(jnp.bfloat16)
    joined = lax.all_to_all(joined_cols, "row", split_axis=0, concat_axis=1, tiled=True)
    pos_h = jnp.zeros((tile_w,), jnp.float32) + (grid_row + offsets[0]).astype(jnp.float32)
    pos_w = (grid_col + offsets[1]).astype(jnp.float32)
    cosine_table, sine_table = rope_tables(pos_h, pos_w, head_size)
    queries = norm_rope(joined[:, :width], q_gain, cosine_table, sine_table, head_count, head_size)
    image_keys = norm_rope(
        joined[:, width : 2 * width], k_gain, cosine_table, sine_table, head_count, head_size
    )
    q_heads, k_heads, v_heads = (
        lax.all_to_all(queries, "col", split_axis=1, concat_axis=0, tiled=True),
        lax.all_to_all(image_keys, "col", split_axis=1, concat_axis=0, tiled=True),
        lax.all_to_all(joined[:, 2 * width :], "col", split_axis=1, concat_axis=0, tiled=True),
    )
    image_rows = k_heads.shape[0]
    text_rows = text_keys.shape[0]
    shard_rows = image_rows + text_rows
    q_block = q_heads.reshape(image_rows, local_heads, head_size)
    key_rows = jnp.concatenate([k_heads, text_keys], 0)
    value_rows = jnp.concatenate([v_heads, text_values], 0)
    run_max = jnp.full((image_rows, local_heads), mask_floor, jnp.float32)
    key_piece = lax.all_gather(key_rows, "row", axis=0, tiled=True)
    value_piece = lax.all_gather(value_rows, "row", axis=0, tiled=True)
    piece_rows = key_piece.shape[0]
    global_row = jnp.arange(piece_rows, dtype=jnp.int32)
    shard_id = global_row // shard_rows
    within = global_row % shard_rows
    is_image = within < image_rows
    source_col = within // tile_w
    source_cell = within % tile_w
    image_req = shard_id % REQ
    text_req = (shard_id * text_rows + within - image_rows) // TXT
    key_req = jnp.where(is_image, image_req, text_req)
    key_onehot = key_req[:, None] == req_slots[None, :]
    key_height = jnp.sum(jnp.where(key_onehot, grid_size[:, 0][None, :], 0), 1)
    key_width = jnp.sum(jnp.where(key_onehot, grid_size[:, 1][None, :], 0), 1)
    image_ok = (shard_id // REQ < key_height) & (source_col * tile_w + source_cell < key_width)
    key_ok = (key_req == request) & (jnp.logical_not(is_image) | image_ok)
    scores = jnp.einsum(
        "qhd,khd->qhk",
        q_block,
        key_piece.reshape(piece_rows, local_heads, head_size),
        preferred_element_type=jnp.float32,
    ) * head_size ** (-0.5)
    new_max = jnp.maximum(run_max, jnp.max(jnp.where(key_ok, scores, mask_floor), -1))
    weights = jnp.where(key_ok, jnp.exp(scores - new_max[..., None]), 0.0)
    new_sum = jnp.sum(weights, -1)
    new_acc = jnp.einsum(
        "qhk,khd->qhd",
        weights.astype(jnp.bfloat16),
        value_piece.reshape(piece_rows, local_heads, head_size),
        preferred_element_type=jnp.float32,
    )
    mixed = (
        (new_acc / new_sum[..., None])
        .astype(jnp.bfloat16)
        .reshape(image_rows, local_heads * head_size)
    )
    partial_out = jnp.dot(
        mixed, lax.all_gather(w_out, "row", axis=1, tiled=True), preferred_element_type=jnp.float32
    )
    attended = lax.psum_scatter(
        partial_out.astype(jnp.bfloat16), "col", scatter_dimension=0, tiled=True
    ).astype(jnp.float32)
    first_res = (states + modulation[2] * attended).astype(jnp.bfloat16)
    normed_two = modulate(first_res.astype(jnp.float32), modulation[3], modulation[4])
    all_rows = lax.all_gather(normed_two, "row", axis=0, tiled=True)
    hidden = jax.nn.gelu(
        jnp.dot(all_rows, w_fc1, preferred_element_type=jnp.float32), approximate=True
    ).astype(jnp.bfloat16)
    every_term = jnp.dot(hidden, w_fc2, preferred_element_type=jnp.float32)
    every_sum = lax.psum(every_term, "row")
    mlp_out = lax.dynamic_slice_in_dim(every_sum, row_pos * tile_w, tile_w, 0)
    second_res = first_res.astype(jnp.float32) + modulation[5] * mlp_out
    normed_three = modulate(second_res, modulation[6], modulation[7])
    raw_velocity = jnp.dot(normed_three, w_final, preferred_element_type=jnp.float32)
    masked = jnp.where(token_ok[:, None], raw_velocity, 0.0)
    padded = with_halo(masked, (("col", 0),), 1)
    left_side = padded[:-2]
    right_side = padded[2:]
    velocity = jnp.where(
        token_ok[:, None], masked + blend * (left_side + right_side - 2.0 * masked), 0.0
    )
    next_latent = latent + -1.0 / STEPS * velocity
    return (velocity, next_latent)


def solution(mesh):
    placed = (
        P(("row", "col"), None),
        P(("row", "col"), None),
        P("row", "col"),
        P("row", "col"),
        P(),
        P(),
        P(),
        P(),
        P(None, "row"),
        P(),
        P(),
        P("col", "row"),
        P(None, "row"),
        P("row", None),
        P(),
    )
    return jax.shard_map(
        on_device,
        mesh=mesh,
        in_specs=placed,
        out_specs=(P(("row", "col"), None), P(("row", "col"), None)),
        check_vma=False,
    )
```

profile of v0, /device:TPU:1, one launch (start us, length us, event | category | flops | bytes accessed | tf_op | source)
XLA Modules:
  0.0 413.6 jit_solution(1863781639350607465)
XLA Ops:
  12.3 2.2 dynamic-slice_add_fusion
  15.3 25.6 %all-gather = bf16[8,2,3072]{2,1,0:T(2,128)(2,1)S(1)} all-gather(bf16[1,2,3072]{2,1,0:T(2,128)(2,1)S(1)} %fusion.50), channel_id=1, replica_groups=mesh['row'=8,'col'=4] {'row'}, dimensions={0}, use_global_device_ids=true | all-gather | bytes 110592 | tf_op jit(solution)/shard_map/all_gather | solution.py:112
  41.0 4.0 convolution_convert_fusion.1
  45.7 5.0 %all-to-all-start = ((bf16[8,2,1152]{2,1,0:T(2,128)(2,1)}), bf16[8,2,1152]{2,1,0:T(2,128)(2,1)S(1)}, u32[]{:S(2)}, u32[]{:S(2)}) async-start(bf16[8,2,1152]{2,1,0:T(2,128)(2,1)} %all_to_all.50), calls=%async_computation | async-start | bytes 73728 | tf_op jit(solution)/shard_map/all_to_all | solution.py:114
  59.2 2.3 reshape.264
  63.3 5.2 %slice_multiply_fusion.5 = (f32[2,24,64,1]{3,2,1,0:T(8,128)}, f32[2,24,64,1]{3,2,1,0:T(8,128)}, f32[2,24,64,1]{3,2,1,0:T(8,128)}, f32[2,24,64,1]{3,2,1,0:T(8,128...) fusion(f32[2,24,64,2]{3,2,1,0:T(8,128)S(1)} %multiply_multiply_, ...), kind=kLoop, calls=%fused_computation.11 | loop fusion | flops 24576 | bytes 148480 | tf_op jit(solution)/shard_map/mul | solution.py:69
  68.5 2.5 copy.52
  71.1 2.5 copy.53
  73.6 2.5 copy.54
  76.1 2.5 copy.55
  80.8 2.0 copy.56
  82.8 2.1 convert_element_type.69
  84.9 14.5 %all_to_all.67 = bf16[2,4,768]{2,0,1:T(2,128)(2,1)} all-to-all(bf16[2,4,768]{2,0,1:T(2,128)(2,1)S(1)} %copy.57), channel_id=1, replica_groups=mesh['row'=8,'col'=4] {'col'}, dimensions={1} | all-to-all | bytes 24576 | tf_op jit(solution)/shard_map/all_to_all | solution.py:124
  101.8 7.8 %all_to_all.68 = bf16[2,4,768]{2,0,1:T(2,128)(2,1)} all-to-all(bf16[2,4,768]{2,0,1:T(2,128)(2,1)} %bitcast.72), channel_id=1, replica_groups=mesh['row'=8,'col'=4] {'col'}, dimensions={1} | all-to-all | bytes 24576 | tf_op jit(solution)/shard_map/all_to_all | solution.py:125
  112.8 2.5 copy.59
  115.4 2.5 copy.60
  121.9 3.9 all-to-all-start.3
  127.2 2.2 all-to-all-done.3
  129.4 14.7 %all-gather.8.cloned.1.call-done = bf16[1088,768]{1,0:T(8,128)(2,1)} async-done(((bf16[136,768]{1,0:T(8,128)(2,1)}), bf16[1088,768]{1,0:T(8,128)(2,1)}) %all-gather.8.cloned.1.call-update) | async-done | bytes 1671184 | tf_op jit(solution)/shard_map/all_gather | solution.py:134
  144.1 3.8 copy.58
  147.9 42.3 %all-gather.6.cloned.1.call-done = bf16[1088,768]{1,0:T(8,128)(2,1)} async-done(((bf16[136,768]{1,0:T(8,128)(2,1)}), bf16[1088,768]{1,0:T(8,128)(2,1)}) %all-gather.6.cloned.1.call-update) | async-done | bytes 1671184 | tf_op jit(solution)/shard_map/all_gather | solution.py:135
  190.2 2.7 copy.51
  192.9 1.9 select_reduce_fusion
  195.0 77.3 %all-gather.10.cloned.1.call-done = bf16[768,3072]{1,0:T(8,128)(2,1)} async-done(((bf16[768,384]{1,0:T(8,128)(2,1)}), bf16[768,3072]{1,0:T(8,128)(2,1)}) %all-gather.10.cloned.1.call-update) | async-done | bytes 4718608 | tf_op jit(solution)/shard_map/all_gather | solution.py:172
  272.3 3.7 convolution_convert_fusion
  276.0 11.2 %all-reduce = bf16[8,3072]{1,0:T(8,128)(2,1)S(1)} all-reduce(bf16[8,3072]{1,0:T(8,128)(2,1)S(1)} %convolution_convert_fusion), channel_id=2, replica_groups=mesh['row'=8,'col'=4] {'col'}, use_global_device_ids=true, to_apply=%region_11.12.clone | all-reduce | flops 24576 | bytes 98304
  287.7 24.4 %all-gather.1 = bf16[8,2,3072]{2,1,0:T(2,128)(2,1)S(1)} all-gather(bf16[1,2,3072]{2,1,0:T(2,128)(2,1)S(1)} %fusion.51), channel_id=1, replica_groups=mesh['row'=8,'col'=4] {'row'}, dimensions={0}, use_global_device_ids=true | all-gather | bytes 110592 | tf_op jit(solution)/shard_map/all_gather | solution.py:179
  312.2 9.6 %fusion.22 = f32[16,3072]{1,0:T(8,128)} fusion(bf16[1536,3072]{1,0:T(8,128)(2,1)} %param.28, bf16[16,3072]{1,0:T(8,128)(2,1)S(1)} %reshape.272, bf16[3072,1536]{1,0:T(8,128)(2,1)} %param.27), kind=kOutput, calls=%fused_computation.37 | convolution fusion | flops 302211072 | bytes 19169280 | tf_op jit(solution)/shard_map/dot_general | solution.py:183
  323.0 71.4 %all-reduce.3.cloned.1.call-done = f32[16,3072]{1,0:T(8,128)} async-done(((f32[16,3072]{1,0:T(8,128)}), f32[16,3072]{1,0:T(8,128)}) %all-reduce.3.cloned.1.call-update) | async-done | bytes 196624 | tf_op jit(solution)/shard_map/psum | solution.py:184
  396.0 5.6 %collective-permute-start = (f32[1,64]{1,0:T(1,128)S(1)}, f32[1,64]{1,0:T(1,128)S(1)}, u32[]{:S(2)}, u32[]{:S(2)}) collective-permute-start(f32[1,64]{1,0:T(1,128)S(1)} %get-tuple-element.45), channel_id=1, source_target_pairs={{0,1},{1,2},{2,3},{4,5},{5,6},{6,7},{8,9},{9,10},{10,11},{12,13},{... | collective-permute-start | bytes 776 | tf_op jit(solution)/shard_map/ppermute | solution.py:22
  401.5 1.9 collective-permute-start.1
  403.5 2.9 collective-permute-done.1
  (113 shorter events, 30.2 us)
Async XLA Ops:
  7.2 388.5 %copy-start = (bf16[3072,64]{0,1:T(8,128)(2,1)S(1)}, bf16[3072,64]{0,1:T(8,128)(2,1)}, u32[]{:S(2)}) copy-start(bf16[3072,64]{0,1:T(8,128)(2,1)} %param.29) | copy-start | bytes 1179652
  41.0 9.8 %copy-start.12 = (s32[4,2]{0,1:T(2,128)S(1)}, s32[4,2]{0,1:T(2,128)}, u32[]{:S(2)}) copy-start(s32[4,2]{0,1:T(2,128)} %param.21) | copy-start | bytes 100
  41.0 9.8 %copy-start.13 = (s32[4,2]{0,1:T(2,128)S(1)}, s32[4,2]{0,1:T(2,128)}, u32[]{:S(2)}) copy-start(s32[4,2]{0,1:T(2,128)} %param.22) | copy-start | bytes 100
  41.0 12.1 %copy-start.15 = (f32[128]{0:T(128)S(1)}, f32[128]{0:T(128)}, u32[]{:S(2)}) copy-start(f32[128]{0:T(128)} %param.24) | copy-start | bytes 1540
  41.0 12.9 %copy-start.16 = (f32[128]{0:T(128)S(1)}, f32[128]{0:T(128)}, u32[]{:S(2)}) copy-start(f32[128]{0:T(128)} %param.25) | copy-start | bytes 1540
  45.7 10.6 %all-to-all-start = ((bf16[8,2,1152]{2,1,0:T(2,128)(2,1)}), bf16[8,2,1152]{2,1,0:T(2,128)(2,1)S(1)}, u32[]{:S(2)}, u32[]{:S(2)}) async-start(bf16[8,2,1152]{2,1,0:T(2,128)(2,1)} %all_to_all.50), calls=%async_computation | async-start | bytes 73728 | tf_op jit(solution)/shard_map/all_to_all | solution.py:114
  50.7 93.4 %all-gather.8.cloned.1.call-start = ((), (), s32[]{:S(2)}) async-start(), calls=%async_computation.5 | async-start | bytes 1880064 | tf_op jit(solution)/shard_map/all_gather | solution.py:134
  62.2 1.0 copy-start.2
  101.8 88.4 %all-gather.6.cloned.1.call-start = ((), (), s32[]{:S(2)}) async-start(), calls=%async_computation.4 | async-start | bytes 1880064 | tf_op jit(solution)/shard_map/all_gather | solution.py:135
  111.9 160.4 %all-gather.10.cloned.1.call-start = ((), (), s32[]{:S(2)}) async-start(), calls=%async_computation.6 | async-start | bytes 5308416 | tf_op jit(solution)/shard_map/all_gather | solution.py:172
  119.0 0.7 copy-start.3
  119.0 0.8 copy-start.4
  119.0 0.8 copy-start.5
  119.0 6.9 %copy-start.17 = (u32[32]{0:T(128)S(1)}, u32[32]{0:T(128)}, u32[]{:S(2)}) copy-start(u32[32]{0:T(128)} %constant.158) | copy-start | bytes 388
  121.9 7.5 %all-to-all-start.3 = ((bf16[2,4,768]{2,0,1:T(2,128)(2,1)}), bf16[2,4,768]{2,0,1:T(2,128)(2,1)S(1)}, u32[]{:S(2)}, u32[]{:S(2)}) async-start(bf16[2,4,768]{2,0,1:T(2,128)(2,1)} %copy.64), calls=%async_computation.3 | async-start | bytes 24576 | tf_op jit(solution)/shard_map/all_to_all | solution.py:123
  125.9 268.5 %all-reduce.3.cloned.1.call-start = ((), (), s32[]{:S(2)}) async-start(), calls=%async_computation.7 | async-start | bytes 393216 | tf_op jit(solution)/shard_map/psum | solution.py:184
  272.3 14.9 %copy-start.1 = (bf16[2,3072]{1,0:T(2,128)(2,1)S(1)}, bf16[2,3072]{1,0:T(2,128)(2,1)}, u32[]{:S(2)}) copy-start(bf16[2,3072]{1,0:T(2,128)(2,1)} %param.15) | copy-start | bytes 36868
  272.3 14.9 %copy-start.9 = (f32[1,1,3072]{2,1,0:T(1,128)S(1)}, f32[1,1,3072]{2,1,0:T(1,128)}, u32[]{:S(2)}) copy-start(f32[1,1,3072]{2,1,0:T(1,128)} %get-tuple-element.30) | copy-start | bytes 36868
  272.3 15.3 %copy-start.7 = (f32[1,1,3072]{2,1,0:T(1,128)S(1)}, f32[1,1,3072]{2,1,0:T(1,128)}, u32[]{:S(2)}) copy-start(f32[1,1,3072]{2,1,0:T(1,128)} %get-tuple-element.25) | copy-start | bytes 36868
  272.3 15.3 %copy-start.8 = (f32[1,1,3072]{2,1,0:T(1,128)S(1)}, f32[1,1,3072]{2,1,0:T(1,128)}, u32[]{:S(2)}) copy-start(f32[1,1,3072]{2,1,0:T(1,128)} %get-tuple-element.26) | copy-start | bytes 36868
  312.1 82.3 %copy-start.6 = (f32[1,1,3072]{2,1,0:T(1,128)S(1)}, f32[1,1,3072]{2,1,0:T(1,128)}, u32[]{:S(2)}) copy-start(f32[1,1,3072]{2,1,0:T(1,128)} %get-tuple-element.27) | copy-start | bytes 36868
  312.1 83.6 %copy-start.10 = (f32[1,1,3072]{2,1,0:T(1,128)S(1)}, f32[1,1,3072]{2,1,0:T(1,128)}, u32[]{:S(2)}) copy-start(f32[1,1,3072]{2,1,0:T(1,128)} %get-tuple-element.24) | copy-start | bytes 36868
  312.1 83.6 %copy-start.11 = (f32[1,1,3072]{2,1,0:T(1,128)S(1)}, f32[1,1,3072]{2,1,0:T(1,128)}, u32[]{:S(2)}) copy-start(f32[1,1,3072]{2,1,0:T(1,128)} %get-tuple-element.31) | copy-start | bytes 36868
  312.1 94.3 %copy-start.14 = (f32[2,64]{1,0:T(2,128)S(1)}, f32[2,64]{1,0:T(2,128)}, u32[]{:S(2)}) copy-start(f32[2,64]{1,0:T(2,128)} %param.16) | copy-start | bytes 1540
  396.0 7.5 %collective-permute-start = (f32[1,64]{1,0:T(1,128)S(1)}, f32[1,64]{1,0:T(1,128)S(1)}, u32[]{:S(2)}, u32[]{:S(2)}) collective-permute-start(f32[1,64]{1,0:T(1,128)S(1)} %get-tuple-element.45), channel_id=1, source_target_pairs={{0,1},{1,2},{2,3},{4,5},{5,6},{6,7},{8,9},{9,10},{10,11},{12,13},{... | collective-permute-start | bytes 776 | tf_op jit(solution)/shard_map/ppermute | solution.py:22
  401.5 4.9 %collective-permute-start.1 = (f32[1,64]{1,0:T(1,128)S(1)}, f32[1,64]{1,0:T(1,128)S(1)}, u32[]{:S(2)}, u32[]{:S(2)}) collective-permute-start(f32[1,64]{1,0:T(1,128)S(1)} %get-tuple-element.46), channel_id=1, source_target_pairs={{1,0},{2,1},{3,2},{5,4},{6,5},{7,6},{9,8},{10,9},{11,10},{13,12},{... | collective-permute-start | bytes 776 | tf_op jit(solution)/shard_map/ppermute | solution.py:24
Sparse Core Ops, SparseCore 0:
  101.9 42.1 all-gather.7
  146.3 43.8 all-gather.5
  192.3 79.9 all-gather.9
  321.9 72.4 all-reduce.2
where the time goes:
time: 415 us; the launch traced here: 414 us
  waiting for transfers between devices  213 us (51%)
  blocking collectives  83.5 us (20%)
  local copies, waits for them, and re-layouts  38.6 us (9%)
  other arithmetic  24.4 us (6%)
  matrix products  19.5 us (5%)
  between operations  18 us (4%)
  starting transfers between devices  16.5 us (4%)
    all_gather x1, waiting for transfers between devices, on_device(): lax.all_gather(w_out, 'row', axis=1, tiled=True)  77.3 us
    psum x1, waiting for transfers between devices, on_device(): every_sum = lax.psum(every_term, 'row')  71.4 us
    all_gather x1, waiting for transfers between devices, on_device(): value_piece = lax.all_gather(value_rows, 'row', axis=0, tiled=True)  42.3 us
    all_gather x1, blocking collectives, on_device(): lax.all_gather(normed, 'row', axis=0, tiled=True)  25.6 us
    all_gather x1, blocking collectives, on_device(): all_rows = lax.all_gather(normed_two, 'row', axis=0, tiled=True)  24.4 us
    all_gather x1, waiting for transfers between devices, on_device(): key_piece = lax.all_gather(key_rows, 'row', axis=0, tiled=True)  14.7 us
    all_to_all x1, blocking collectives, on_device(): lax.all_to_all(image_keys, 'col', split_axis=1, concat_axis=0, tiled=True)  14.5 us
    unnamed x1, blocking collectives  11.2 us
  transfers between devices with their start and end apart: 8, of which 7 were waited for; matrix products, arithmetic and copies ran while one was open for 6% of the time, Pallas kernels for 0%

commit v1 on v0

--- a/solution.py
+++ b/solution.py
@@ -131,8 +131,11 @@
     key_rows = jnp.concatenate([k_heads, text_keys], 0)
     value_rows = jnp.concatenate([v_heads, text_values], 0)
     run_max = jnp.full((image_rows, local_heads), mask_floor, jnp.float32)
-    key_piece = lax.all_gather(key_rows, "row", axis=0, tiled=True)
-    value_piece = lax.all_gather(value_rows, "row", axis=0, tiled=True)
+    key_piece, value_piece = jnp.split(
+        lax.all_gather(jnp.concatenate([key_rows, value_rows], axis=1), "row", axis=0, tiled=True),
+        [key_rows.shape[1]],
+        axis=1,
+    )
     piece_rows = key_piece.shape[0]
     global_row = jnp.arange(piece_rows, dtype=jnp.int32)
     shard_id = global_row // shard_rows

time: 415 us -> 398 us (0.959)
  waiting for transfers between devices: 213 us -> 194 us
  blocking collectives: 83.5 us -> 75.8 us
  local copies, waits for them, and re-layouts: 38.6 us -> 43.5 us
  starting transfers between devices: 16.5 us -> 20.9 us
    all_gather x2 -> x1, waiting for transfers between devices: 56.9 us -> 42.1 us  [on_device(): lax.all_gather(jnp.concatenate([key_rows, value_rows], axis=1), 'row', ax...]
    split x0 -> x3, local copies, waits for them, and re-layouts: none -> 8.37 us  [on_device(): jnp.split(lax.all_gather(jnp.concatenate([key_rows, value_rows], axis=1),...]
    all_to_all x1 -> x0, blocking collectives: 7.75 us -> none  [on_device(): lax.all_to_all(joined[:, 2 * width:], 'col', split_axis=1, concat_axis=0,...]
    all_gather x2 -> x0, local copies, waits for them, and re-layouts: 6.55 us -> none  [the longest x1 3.84 us: on_device(): key_piece = lax.all_gather(key_rows, 'row', axis=0, tiled=True)]
    all_gather x1, waiting for transfers between devices: 77.3 us -> 71.7 us  [on_device(): lax.all_gather(w_out, 'row', axis=1, tiled=True)]
    all_to_all x0 -> x1, starting transfers between devices: none -> 4.38 us  [on_device(): lax.all_to_all(joined[:, 2 * width:], 'col', split_axis=1, concat_axis=0,...]
where the time goes in v1:
time: 398 us; the launch traced here: 397 us
  waiting for transfers between devices  194 us (49%)
  blocking collectives  75.8 us (19%)
  local copies, waits for them, and re-layouts  43.5 us (11%)
  other arithmetic  24.8 us (6%)
  starting transfers between devices  20.9 us (5%)
  matrix products  19.6 us (5%)
  between operations  18 us (5%)
    all_gather x1, waiting for transfers between devices, on_device(): lax.all_gather(w_out, 'row', axis=1, tiled=True)  71.7 us
    psum x1, waiting for transfers between devices, on_device(): every_sum = lax.psum(every_term, 'row')  71.4 us
    all_gather x1, waiting for transfers between devices, on_device(): lax.all_gather(jnp.concatenate([key_rows, value_rows], axis=1), 'row', ax...  42.1 us
    all_gather x1, blocking collectives, on_device(): lax.all_gather(normed, 'row', axis=0, tiled=True)  25.6 us
    all_gather x1, blocking collectives, on_device(): all_rows = lax.all_gather(normed_two, 'row', axis=0, tiled=True)  24.4 us
    all_to_all x1, blocking collectives, on_device(): lax.all_to_all(image_keys, 'col', split_axis=1, concat_axis=0, tiled=True)  14.5 us
    unnamed x1, blocking collectives  11.2 us
    dot_general x1, matrix products, on_device(): every_term = jnp.dot(hidden, w_fc2, preferred_element_type=jnp.float32)  9.62 us
  transfers between devices with their start and end apart: 8, of which 7 were waited for; matrix products, arithmetic and copies ran while one was open for 6% of the time, Pallas kernels for 0%

profile of v1, /device:TPU:1, one launch (start us, length us, event | category | flops | bytes accessed | tf_op | source)
XLA Modules:
  0.0 396.6 jit_solution(10871724446155968353)
XLA Ops:
  12.3 2.2 dynamic-slice_add_fusion
  15.3 25.6 %all-gather = bf16[8,2,3072]{2,1,0:T(2,128)(2,1)S(1)} all-gather(bf16[1,2,3072]{2,1,0:T(2,128)(2,1)S(1)} %fusion.50), channel_id=1, replica_groups=mesh['row'=8,'col'=4] {'row'}, dimensions={0}, use_global_device_ids=true | all-gather | bytes 110592 | tf_op jit(solution)/shard_map/all_gather | solution.py:112
  41.0 4.0 %convolution_convert_fusion.1 = bf16[16,1152]{1,0:T(8,128)(2,1)S(1)} fusion(bf16[16,3072]{1,0:T(8,128)(2,1)S(1)} %reshape.270, bf16[3072,1152]{1,0:T(8,128)(2,1)} %param.23), kind=kOutput, calls=%fused_computation.3 | convolution fusion | flops 113264640 | bytes 7213056 | tf_op jit(solution)/shard_map/dot_general | solution.py:111
  45.7 5.0 %all-to-all-start = ((bf16[8,2,1152]{2,1,0:T(2,128)(2,1)}), bf16[8,2,1152]{2,1,0:T(2,128)(2,1)S(1)}, u32[]{:S(2)}, u32[]{:S(2)}) async-start(bf16[8,2,1152]{2,1,0:T(2,128)(2,1)} %all_to_all.50), calls=%async_computation | async-start | bytes 73728 | tf_op jit(solution)/shard_map/all_to_all | solution.py:114
  59.8 2.3 reshape.263
  64.4 5.3 %slice_multiply_fusion.5 = (f32[2,24,64,1]{3,2,1,0:T(8,128)}, f32[2,24,64,1]{3,2,1,0:T(8,128)}, f32[2,24,64,1]{3,2,1,0:T(8,128)}, f32[2,24,64,1]{3,2,1,0:T(8,128...) fusion(f32[2,24,64,2]{3,2,1,0:T(8,128)S(1)} %multiply_multiply_, ...), kind=kLoop, calls=%fused_computation.11 | loop fusion | flops 24576 | bytes 148480 | tf_op jit(solution)/shard_map/mul | solution.py:69
  69.7 2.5 copy.50
  72.2 2.5 copy.51
  74.8 2.5 copy.52
  77.3 2.5 copy.53
  82.0 2.0 copy.54
  84.0 2.7 convert_element_type.69
  87.4 14.5 %all_to_all.67 = bf16[2,4,768]{2,0,1:T(2,128)(2,1)} all-to-all(bf16[2,4,768]{2,0,1:T(2,128)(2,1)S(1)} %copy.55), channel_id=1, replica_groups=mesh['row'=8,'col'=4] {'col'}, dimensions={1} | all-to-all | bytes 24576 | tf_op jit(solution)/shard_map/all_to_all | solution.py:124
  101.9 4.4 %all-to-all-start.2 = ((bf16[2,4,768]{2,0,1:T(2,128)(2,1)}), bf16[2,4,768]{2,0,1:T(2,128)(2,1)}, u32[]{:S(2)}, u32[]{:S(2)}) async-start(bf16[2,4,768]{2,0,1:T(2,128)(2,1)} %bitcast.72), calls=%async_computation.2 | async-start | bytes 24576 | tf_op jit(solution)/shard_map/all_to_all | solution.py:125
  114.2 2.5 copy.59
  116.7 2.5 copy.60
  123.3 4.0 all-to-all-start.3
  128.6 2.2 all-to-all-done.3
  130.8 42.1 %all-gather.5.cloned.1.call-done = bf16[1088,1536]{1,0:T(8,128)(2,1)} async-done(((bf16[136,1536]{1,0:T(8,128)(2,1)}), bf16[1088,1536]{1,0:T(8,128)(2,1)}) %all-gather.5.cloned.1.call-update) | async-done | bytes 3342352 | tf_op jit(solution)/shard_map/all_gather | solution.py:135
  173.0 3.4 fusion.84
  176.4 2.2 copy.58
  178.6 2.7 copy.57
  181.3 2.0 select_reduce_fusion
  183.6 71.7 %all-gather.7.cloned.1.call-done = bf16[768,3072]{1,0:T(8,128)(2,1)} async-done(((bf16[768,384]{1,0:T(8,128)(2,1)}), bf16[768,3072]{1,0:T(8,128)(2,1)}) %all-gather.7.cloned.1.call-update) | async-done | bytes 4718608 | tf_op jit(solution)/shard_map/all_gather | solution.py:175
  255.3 3.7 convolution_convert_fusion
  259.0 11.2 %all-reduce = bf16[8,3072]{1,0:T(8,128)(2,1)S(1)} all-reduce(bf16[8,3072]{1,0:T(8,128)(2,1)S(1)} %convolution_convert_fusion), channel_id=2, replica_groups=mesh['row'=8,'col'=4] {'col'}, use_global_device_ids=true, to_apply=%region_11.12.clone | all-reduce | flops 24576 | bytes 98304
  270.7 24.4 %all-gather.1 = bf16[8,2,3072]{2,1,0:T(2,128)(2,1)S(1)} all-gather(bf16[1,2,3072]{2,1,0:T(2,128)(2,1)S(1)} %fusion.51), channel_id=1, replica_groups=mesh['row'=8,'col'=4] {'row'}, dimensions={0}, use_global_device_ids=true | all-gather | bytes 110592 | tf_op jit(solution)/shard_map/all_gather | solution.py:182
  295.2 9.6 %fusion.22 = f32[16,3072]{1,0:T(8,128)} fusion(bf16[1536,3072]{1,0:T(8,128)(2,1)} %param.28, bf16[16,3072]{1,0:T(8,128)(2,1)S(1)} %reshape.272, bf16[3072,1536]{1,0:T(8,128)(2,1)} %param.27), kind=kOutput, calls=%fused_computation.36 | convolution fusion | flops 302211072 | bytes 19169280 | tf_op jit(solution)/shard_map/dot_general | solution.py:186
  306.0 71.4 %all-reduce.3.cloned.1.call-done = f32[16,3072]{1,0:T(8,128)} async-done(((f32[16,3072]{1,0:T(8,128)}), f32[16,3072]{1,0:T(8,128)}) %all-reduce.3.cloned.1.call-update) | async-done | bytes 196624 | tf_op jit(solution)/shard_map/psum | solution.py:187
  379.0 5.6 %collective-permute-start = (f32[1,64]{1,0:T(1,128)S(1)}, f32[1,64]{1,0:T(1,128)S(1)}, u32[]{:S(2)}, u32[]{:S(2)}) collective-permute-start(f32[1,64]{1,0:T(1,128)S(1)} %get-tuple-element.47), channel_id=1, source_target_pairs={{0,1},{1,2},{2,3},{4,5},{5,6},{6,7},{8,9},{9,10},{10,11},{12,13},{... | collective-permute-start | bytes 776 | tf_op jit(solution)/shard_map/ppermute | solution.py:22
  384.6 1.9 collective-permute-start.1
  386.5 2.9 collective-permute-done.1
  (117 shorter events, 34.2 us)
Async XLA Ops:
  7.2 371.5 %copy-start = (bf16[3072,64]{0,1:T(8,128)(2,1)S(1)}, bf16[3072,64]{0,1:T(8,128)(2,1)}, u32[]{:S(2)}) copy-start(bf16[3072,64]{0,1:T(8,128)(2,1)} %param.29) | copy-start | bytes 1179652
  41.0 9.8 %copy-start.14 = (s32[4,2]{0,1:T(2,128)S(1)}, s32[4,2]{0,1:T(2,128)}, u32[]{:S(2)}) copy-start(s32[4,2]{0,1:T(2,128)} %param.21) | copy-start | bytes 100
  41.0 9.8 %copy-start.16 = (s32[4,2]{0,1:T(2,128)S(1)}, s32[4,2]{0,1:T(2,128)}, u32[]{:S(2)}) copy-start(s32[4,2]{0,1:T(2,128)} %param.22) | copy-start | bytes 100
  41.0 12.7 %copy-start.18 = (f32[128]{0:T(128)S(1)}, f32[128]{0:T(128)}, u32[]{:S(2)}) copy-start(f32[128]{0:T(128)} %param.24) | copy-start | bytes 1540
  41.0 13.4 %copy-start.19 = (f32[128]{0:T(128)S(1)}, f32[128]{0:T(128)}, u32[]{:S(2)}) copy-start(f32[128]{0:T(128)} %param.25) | copy-start | bytes 1540
  45.7 10.6 %all-to-all-start = ((bf16[8,2,1152]{2,1,0:T(2,128)(2,1)}), bf16[8,2,1152]{2,1,0:T(2,128)(2,1)S(1)}, u32[]{:S(2)}, u32[]{:S(2)}) async-start(bf16[8,2,1152]{2,1,0:T(2,128)(2,1)} %all_to_all.50), calls=%async_computation | async-start | bytes 73728 | tf_op jit(solution)/shard_map/all_to_all | solution.py:114
  62.8 1.0 copy-start.2
  63.7 0.7 copy-start.13
  84.0 29.5 %copy-start.15 = (s32[4,2]{0,1:T(2,128)S(1)}, s32[4,2]{0,1:T(2,128)}, u32[]{:S(2)}) copy-start(s32[4,2]{0,1:T(2,128)} %param.21) | copy-start | bytes 100
  101.9 7.6 %all-to-all-start.2 = ((bf16[2,4,768]{2,0,1:T(2,128)(2,1)}), bf16[2,4,768]{2,0,1:T(2,128)(2,1)}, u32[]{:S(2)}, u32[]{:S(2)}) async-start(bf16[2,4,768]{2,0,1:T(2,128)(2,1)} %bitcast.72), calls=%async_computation.2 | async-start | bytes 24576 | tf_op jit(solution)/shard_map/all_to_all | solution.py:125
  106.3 66.7 %all-gather.5.cloned.1.call-start = ((), (), s32[]{:S(2)}) async-start(), calls=%async_computation.4 | async-start | bytes 3760128 | tf_op jit(solution)/shard_map/all_gather | solution.py:135
  112.7 142.6 %all-gather.7.cloned.1.call-start = ((), (), s32[]{:S(2)}) async-start(), calls=%async_computation.5 | async-start | bytes 5308416 | tf_op jit(solution)/shard_map/all_gather | solution.py:175
  120.4 0.7 copy-start.3
  120.4 0.8 copy-start.4
  120.4 0.8 copy-start.5
  120.4 6.9 %copy-start.9 = (s32[1088]{0:T(1024)S(1)}, s32[1088]{0:T(1024)}, u32[]{:S(2)}) copy-start(s32[1088]{0:T(1024)} %get-tuple-element.2) | copy-start | bytes 13060
  120.4 6.9 %copy-start.10 = (s32[1088]{0:T(1024)S(1)}, s32[1088]{0:T(1024)}, u32[]{:S(2)}) copy-start(s32[1088]{0:T(1024)} %get-tuple-element.3) | copy-start | bytes 13060
  120.4 6.9 %copy-start.20 = (u32[32]{0:T(128)S(1)}, u32[32]{0:T(128)}, u32[]{:S(2)}) copy-start(u32[32]{0:T(128)} %constant.158) | copy-start | bytes 388
  123.3 7.5 %all-to-all-start.3 = ((bf16[2,4,768]{2,0,1:T(2,128)(2,1)}), bf16[2,4,768]{2,0,1:T(2,128)(2,1)S(1)}, u32[]{:S(2)}, u32[]{:S(2)}) async-start(bf16[2,4,768]{2,0,1:T(2,128)(2,1)} %copy.64), calls=%async_computation.3 | async-start | bytes 24576 | tf_op jit(solution)/shard_map/all_to_all | solution.py:123
  127.3 250.1 %all-reduce.3.cloned.1.call-start = ((), (), s32[]{:S(2)}) async-start(), calls=%async_computation.6 | async-start | bytes 393216 | tf_op jit(solution)/shard_map/psum | solution.py:187
  255.3 14.9 %copy-start.1 = (bf16[2,3072]{1,0:T(2,128)(2,1)S(1)}, bf16[2,3072]{1,0:T(2,128)(2,1)}, u32[]{:S(2)}) copy-start(bf16[2,3072]{1,0:T(2,128)(2,1)} %param.15) | copy-start | bytes 36868
  255.3 14.9 %copy-start.8 = (f32[1,1,3072]{2,1,0:T(1,128)S(1)}, f32[1,1,3072]{2,1,0:T(1,128)}, u32[]{:S(2)}) copy-start(f32[1,1,3072]{2,1,0:T(1,128)} %get-tuple-element.32) | copy-start | bytes 36868
  255.3 15.3 %copy-start.6 = (f32[1,1,3072]{2,1,0:T(1,128)S(1)}, f32[1,1,3072]{2,1,0:T(1,128)}, u32[]{:S(2)}) copy-start(f32[1,1,3072]{2,1,0:T(1,128)} %get-tuple-element.27) | copy-start | bytes 36868
  255.3 15.3 %copy-start.7 = (f32[1,1,3072]{2,1,0:T(1,128)S(1)}, f32[1,1,3072]{2,1,0:T(1,128)}, u32[]{:S(2)}) copy-start(f32[1,1,3072]{2,1,0:T(1,128)} %get-tuple-element.28) | copy-start | bytes 36868
  295.1 83.6 %copy-start.11 = (f32[1,1,3072]{2,1,0:T(1,128)S(1)}, f32[1,1,3072]{2,1,0:T(1,128)}, u32[]{:S(2)}) copy-start(f32[1,1,3072]{2,1,0:T(1,128)} %get-tuple-element.26) | copy-start | bytes 36868
  295.2 83.6 %copy-start.12 = (f32[1,1,3072]{2,1,0:T(1,128)S(1)}, f32[1,1,3072]{2,1,0:T(1,128)}, u32[]{:S(2)}) copy-start(f32[1,1,3072]{2,1,0:T(1,128)} %get-tuple-element.33) | copy-start | bytes 36868
  295.2 94.3 %copy-start.17 = (f32[2,64]{1,0:T(2,128)S(1)}, f32[2,64]{1,0:T(2,128)}, u32[]{:S(2)}) copy-start(f32[2,64]{1,0:T(2,128)} %param.16) | copy-start | bytes 1540
  379.0 7.5 %collective-permute-start = (f32[1,64]{1,0:T(1,128)S(1)}, f32[1,64]{1,0:T(1,128)S(1)}, u32[]{:S(2)}, u32[]{:S(2)}) collective-permute-start(f32[1,64]{1,0:T(1,128)S(1)} %get-tuple-element.47), channel_id=1, source_target_pairs={{0,1},{1,2},{2,3},{4,5},{5,6},{6,7},{8,9},{9,10},{10,11},{12,13},{... | collective-permute-start | bytes 776 | tf_op jit(solution)/shard_map/ppermute | solution.py:22
  384.6 4.9 %collective-permute-start.1 = (f32[1,64]{1,0:T(1,128)S(1)}, f32[1,64]{1,0:T(1,128)S(1)}, u32[]{:S(2)}, u32[]{:S(2)}) collective-permute-start(f32[1,64]{1,0:T(1,128)S(1)} %get-tuple-element.48), channel_id=1, source_target_pairs={{1,0},{2,1},{3,2},{5,4},{6,5},{7,6},{9,8},{10,9},{11,10},{13,12},{... | collective-permute-start | bytes 776 | tf_op jit(solution)/shard_map/ppermute | solution.py:24
Sparse Core Ops, SparseCore 0:
  112.8 60.0 all-gather.4
  175.0 80.2 all-gather.6
  304.9 72.4 all-reduce.2
